TPU v7x, 32 devices: a whole 2x2x4 slice. The times are simulated.
32 devices in a mesh: head: 4 (over x, core), blk: 8 (over z, y).
Axes of the slice: x: 2, y: 2, z: 4, core: 2. Of those that a mesh axis runs over, the one named last changes fastest.
Arguments:
- layer_input: bfloat16 [4096, 1024], P(('head', 'blk')), may hold values from -6 to 6
- out_grad: bfloat16 [4096, 1024], P(('head', 'blk')), may hold values from -6 to 6
- lengths: int32 [4], replicated, may hold values from 1 to 2048, 3072 in all
- ln_attn: bfloat16 [1024], P(('head', 'blk')), may hold values from 0.5 to 1.5
- w_qkv: bfloat16 [1024, 3072], P(('head', 'blk')), may hold values from -0.1875 to 0.1875
- w_attn_out: bfloat16 [1024, 1024], P(('head', 'blk')), may hold values from -6 to 6
- ln_mlp: bfloat16 [1024], P(('head', 'blk')), may hold values from 0.5 to 1.5
- w_in: bfloat16 [1024, 5248], P(('head', 'blk')), may hold values from -0.1875 to 0.1875
- w_mlp_out: bfloat16 [2624, 1024], P(None, ('head', 'blk')), may hold values from -0.125 to 0.125
Outputs:
- layer_output: float32 [4096, 1024], P(('head', 'blk'))
- input_grad: float32 [4096, 1024], P(('head', 'blk'))
- d_ln_attn: float32 [1024], P(('head', 'blk'))
- d_w_qkv: float32 [1024, 3072], P(('head', 'blk'))
- d_w_attn_out: float32 [1024, 1024], P(('head', 'blk'))
- d_ln_mlp: float32 [1024], P(('head', 'blk'))
- d_w_in: float32 [1024, 5248], P(('head', 'blk'))
- d_w_mlp_out: float32 [2624, 1024], P(None, ('head', 'blk'))
Inputs may be any that keep to these rules, and one draw needn't show every extreme that they name: lengths of the 4 sequences packed from slot 0; they sum to 3072 and the longest is exactly 2048; the remaining slots are padding.
All inputs are finite; a program needn't handle non-finite values.
Results may differ from a plain program's by a relative error of at most 0.023.
Values may be sent and summed in bfloat16 or wider, within the bound.
A program may use at most 192 MiB of HBM per device.

v0:
```python
import jax
import jax.numpy as jnp
from jax import lax
from jax.sharding import PartitionSpec as P

DH = 64
ROPE_BASE = 160000.0
NORM_EPS = 1e-05
MASK_FLOOR = -1e30


def norm_forward(values, gain):
    centre = values - jnp.mean(values, axis=-1, keepdims=True)
    variance = jnp.mean(centre * centre, axis=-1, keepdims=True)
    scale_row = lax.rsqrt(variance + NORM_EPS)
    normed = centre * scale_row
    return (normed * gain, normed, scale_row)


def norm_backward(grad_rows, gain, normed, scale_row):
    scaled_grad = grad_rows * gain
    gain_grad = jnp.sum(grad_rows * normed, axis=0)
    mean_one = jnp.mean(scaled_grad, axis=-1, keepdims=True)
    mean_two = jnp.mean(scaled_grad * normed, axis=-1, keepdims=True)
    return (scale_row * (scaled_grad - mean_one - normed * mean_two), gain_grad)


def locate(rows_at, lengths):
    seq_ends = jnp.cumsum(lengths)
    segment = jnp.sum((rows_at[:, None] >= seq_ends[None, :]).astype(jnp.int32), axis=1)
    seq_starts = jnp.concatenate([seq_ends - lengths, seq_ends[-1:]])
    picked = segment[:, None] == lax.iota(jnp.int32, seq_starts.shape[0])[None, :]
    begins = jnp.sum(jnp.where(picked, seq_starts[None, :], 0), axis=1)
    return (segment, rows_at - begins)


def rotate(values, position, sign_value):
    half_dim = values.shape[-1] // 2
    inv_freq = jnp.power(ROPE_BASE, -2.0 * lax.iota(jnp.float32, half_dim) / values.shape[-1])
    angles = position.astype(jnp.float32)[:, None] * inv_freq[None, :]
    cosine = jnp.cos(angles)[:, None, :]
    sine_part = sign_value * jnp.sin(angles)[:, None, :]
    front_part = values[..., :half_dim]
    back_part = values[..., half_dim:]
    return jnp.concatenate(
        [front_part * cosine - back_part * sine_part, back_part * cosine + front_part * sine_part],
        axis=-1,
    )


def spread(flat_rows, rows_dev, group_rows, cycle_size):
    owner = flat_rows // group_rows
    inner = flat_rows % group_rows
    return inner // rows_dev * (cycle_size * rows_dev) + owner * rows_dev + inner % rows_dev


def block_size(row_count, base_rows):
    for block_rows in (512, base_rows):
        return block_rows
    return row_count


def take_rows(array_in, block_at, block_rows):
    return lax.dynamic_slice_in_dim(array_in, block_at * block_rows, block_rows, 0)


def online(carried, queries, keys_in, values_in, seg_query, seg_key):
    top_score, row_total, weighted = carried
    scores = (
        jnp.einsum("qhd,khd->hqk", queries, keys_in, preferred_element_type=jnp.float32) * 0.125
    )
    same_seq = (seg_query[:, None] == seg_key[None, :])[None]
    scores = jnp.where(same_seq, scores, MASK_FLOOR)
    new_top = jnp.maximum(top_score, jnp.max(scores, axis=-1))
    weights = jnp.where(same_seq, jnp.exp(scores - new_top[:, :, None]), 0.0)
    rescale = jnp.exp(top_score - new_top)
    row_total = row_total * rescale + jnp.sum(weights, axis=-1)
    weighted = weighted * rescale.T[:, :, None] + jnp.einsum(
        "hqk,khd->qhd", weights.astype(jnp.bfloat16), values_in, preferred_element_type=jnp.float32
    )
    return (new_top, row_total, weighted)


def score_grads(query_in, key_in, value_in, grad_rows, lse_in, delta_in, seg_query, seg_key):
    scores = (
        jnp.einsum("qhd,khd->hqk", query_in, key_in, preferred_element_type=jnp.float32) * 0.125
    )
    same_seq = (seg_query[:, None] == seg_key[None, :])[None]
    probs = jnp.exp(jnp.where(same_seq, scores - lse_in[:, :, None], MASK_FLOOR))
    grad_probs = jnp.einsum("qhd,khd->hqk", grad_rows, value_in, preferred_element_type=jnp.float32)
    grad_scores = (probs * (grad_probs - delta_in[:, :, None])).astype(jnp.bfloat16)
    return (probs, grad_scores)


def key_grad_rows(query_in, grad_rows, lse_in, delta_in, seg_query, keys_in, values_in, seg_key):
    probs, grad_scores = score_grads(
        query_in, keys_in, values_in, grad_rows, lse_in, delta_in, seg_query, seg_key
    )
    grad_keys = 0.125 * jnp.einsum(
        "hqk,qhd->khd", grad_scores, query_in, preferred_element_type=jnp.float32
    )
    grad_values = jnp.einsum(
        "hqk,qhd->khd", probs.astype(jnp.bfloat16), grad_rows, preferred_element_type=jnp.float32
    )
    return (grad_keys, grad_values)


def shards(layer_input, out_grad, lengths, ln_attn, w_qkv, w_attn_out, ln_mlp, w_in, w_mlp_out):
    head_groups = lax.axis_size("head")
    cycle_size = lax.axis_size("blk")
    rows_dev = layer_input.shape[0]
    width = layer_input.shape[1]
    all_heads = width // DH
    local_heads = all_heads // head_groups
    local_width = local_heads * DH
    group_rows = head_groups * rows_dev
    nseq_count = lengths.shape[0]
    gain_one, wqkv_full, wout_full, gain_two, win_full, wdown_full = (
        lax.all_gather(ln_attn, ("head", "blk"), axis=0, tiled=True),
        lax.all_gather(w_qkv, ("head", "blk"), axis=0, tiled=True),
        lax.all_gather(w_attn_out, ("head", "blk"), axis=0, tiled=True),
        lax.all_gather(ln_mlp, ("head", "blk"), axis=0, tiled=True),
        lax.all_gather(w_in, ("head", "blk"), axis=0, tiled=True),
        lax.all_gather(w_mlp_out, ("head", "blk"), axis=1, tiled=True),
    )
    gain_one = gain_one.astype(jnp.float32)
    gain_two = gain_two.astype(jnp.float32)
    blk_index = lax.axis_index("blk")
    own_rows = (lax.axis_index("head") * cycle_size + blk_index) * rows_dev + lax.iota(
        jnp.int32, rows_dev
    )
    segment, position = locate(own_rows, lengths)
    valid = (segment < nseq_count).astype(jnp.float32)[:, None]

    def cycle_segments(first_row, row_count):
        flat_rows = first_row + lax.iota(jnp.int32, row_count)
        return locate(spread(flat_rows, rows_dev, group_rows, cycle_size), lengths)[0]

    x_float = layer_input.astype(jnp.float32)
    norm_one, normed_one, scale_one = norm_forward(x_float, gain_one)
    input_bf = norm_one.astype(jnp.bfloat16)
    qkv_all = jnp.dot(input_bf, wqkv_full, preferred_element_type=jnp.float32).reshape(
        rows_dev, 3, all_heads, DH
    )
    stacked = jnp.stack(
        [rotate(qkv_all[:, 0], position, 1.0), rotate(qkv_all[:, 1], position, 1.0), qkv_all[:, 2]],
        axis=1,
    )
    stacked = stacked.astype(jnp.bfloat16).reshape(rows_dev, 3, head_groups, local_width)
    regrouped = lax.all_to_all(stacked, "head", split_axis=2, concat_axis=0, tiled=True)
    queries = regrouped[:, 0, 0].reshape(group_rows, local_heads, DH)
    key_value = regrouped[:, 1:, 0]
    own_keys = key_value[:, 0].reshape(group_rows, local_heads, DH)
    own_values = key_value[:, 1].reshape(group_rows, local_heads, DH)
    query_seg = cycle_segments(blk_index * group_rows, group_rows)
    start_state = (
        jnp.full((local_heads, group_rows), MASK_FLOOR, jnp.float32),
        jnp.zeros((local_heads, group_rows), jnp.float32),
        jnp.zeros((group_rows, local_heads, DH), jnp.float32),
    )
    carried = start_state
    key_part = lax.all_gather(key_value, "blk", axis=0, tiled=True)
    row_count = key_part.shape[0]
    block_rows = block_size(row_count, group_rows)
    key_seg = cycle_segments(jnp.int32(0), row_count)

    def attend_one_step(inner, block_at):
        part_rows = take_rows(key_part, block_at, block_rows)
        part_seg = take_rows(key_seg, block_at, block_rows)
        keys_in = part_rows[:, 0].reshape(block_rows, local_heads, DH)
        values_in = part_rows[:, 1].reshape(block_rows, local_heads, DH)
        return (online(inner, queries, keys_in, values_in, query_seg, part_seg), None)

    carried, ignored = lax.scan(
        attend_one_step, carried, lax.iota(jnp.int32, row_count // block_rows)
    )
    top_score, row_total, weighted = carried
    log_total = top_score + jnp.log(row_total)
    attended = weighted / row_total.T[:, :, None]
    attended_bf = attended.reshape(group_rows, local_width).astype(jnp.bfloat16)
    mixed = lax.all_to_all(attended_bf, "head", split_axis=0, concat_axis=1, tiled=True)
    attn_out = jnp.dot(mixed, wout_full, preferred_element_type=jnp.float32)
    hidden = x_float + attn_out
    norm_two, normed_two, scale_two = norm_forward(hidden, gain_two)
    middle_bf = norm_two.astype(jnp.bfloat16)
    gate_up = jnp.dot(middle_bf, win_full, preferred_element_type=jnp.float32)
    ff_width = gate_up.shape[1] // 2
    gate_part = gate_up[:, :ff_width]
    up_part = gate_up[:, ff_width:]
    gelu_gate, gelu_pull = jax.vjp(
        lambda gate_in: jax.nn.gelu(gate_in, approximate=False), gate_part
    )
    product = (gelu_gate * up_part).astype(jnp.bfloat16)
    mlp_out = jnp.dot(product, wdown_full, preferred_element_type=jnp.float32)
    y_out = valid * (hidden + mlp_out)
    grad_out = (out_grad.astype(jnp.float32) * valid).astype(jnp.bfloat16)
    grad_down = jnp.dot(product.T, grad_out, preferred_element_type=jnp.float32)
    grad_product = jnp.dot(grad_out, wdown_full.T, preferred_element_type=jnp.float32)
    grad_gate = gelu_pull(grad_product * up_part)[0]
    grad_gate_up = jnp.concatenate([grad_gate, grad_product * gelu_gate], axis=1).astype(
        jnp.bfloat16
    )
    grad_win = jnp.dot(middle_bf.T, grad_gate_up, preferred_element_type=jnp.float32)
    grad_middle = jnp.dot(grad_gate_up, win_full.T, preferred_element_type=jnp.float32)
    grad_hidden_ln, grad_gain_two = norm_backward(grad_middle, gain_two, normed_two, scale_two)
    grad_hidden = grad_out.astype(jnp.float32) + grad_hidden_ln
    grad_attn_bf = grad_hidden.astype(jnp.bfloat16)
    grad_wout = jnp.dot(mixed.T, grad_attn_bf, preferred_element_type=jnp.float32)
    grad_mixed = jnp.dot(grad_attn_bf, wout_full.T, preferred_element_type=jnp.float32).astype(
        jnp.bfloat16
    )
    grad_heads = lax.all_to_all(
        grad_mixed, "head", split_axis=1, concat_axis=0, tiled=True
    ).reshape(group_rows, local_heads, DH)
    row_delta = jnp.sum(grad_heads.astype(jnp.float32) * attended, axis=-1).T
    zero_grad = jnp.zeros((group_rows, local_heads, DH), jnp.float32)
    total_grad = zero_grad
    query_key_part = lax.all_gather(key_value, "blk", axis=0, tiled=True)
    row_count = query_key_part.shape[0]
    query_block_rows = block_size(row_count, group_rows)
    query_key_seg = cycle_segments(jnp.int32(0), row_count)

    def query_one_step(inner, block_at):
        part_rows = take_rows(query_key_part, block_at, query_block_rows)
        part_seg = take_rows(query_key_seg, block_at, query_block_rows)
        keys_in = part_rows[:, 0].reshape(query_block_rows, local_heads, DH)
        values_in = part_rows[:, 1].reshape(query_block_rows, local_heads, DH)
        probs, grad_scores = score_grads(
            queries, keys_in, values_in, grad_heads, log_total, row_delta, query_seg, part_seg
        )
        return (
            inner
            + 0.125
            * jnp.einsum("hqk,khd->qhd", grad_scores, keys_in, preferred_element_type=jnp.float32),
            None,
        )

    total_grad, ignored = lax.scan(
        query_one_step, total_grad, lax.iota(jnp.int32, row_count // query_block_rows)
    )
    carried = (zero_grad, zero_grad)
    query_rows = lax.all_gather(queries.astype(jnp.float32), "blk", axis=0, tiled=True)
    grad_rows = lax.all_gather(grad_heads.astype(jnp.float32), "blk", axis=0, tiled=True)
    lse_rows = lax.all_gather(log_total.T, "blk", axis=0, tiled=True)
    delta_rows = lax.all_gather(row_delta.T, "blk", axis=0, tiled=True)
    row_count = query_rows.shape[0]
    gather_block_rows = block_size(row_count, group_rows)
    seg_rows = cycle_segments(jnp.int32(0), row_count)

    def gather_one_step(inner, block_at):
        grad_keys, grad_values = key_grad_rows(
            take_rows(query_rows, block_at, gather_block_rows).astype(jnp.bfloat16),
            take_rows(grad_rows, block_at, gather_block_rows).astype(jnp.bfloat16),
            take_rows(lse_rows, block_at, gather_block_rows).T,
            take_rows(delta_rows, block_at, gather_block_rows).T,
            take_rows(seg_rows, block_at, gather_block_rows),
            own_keys,
            own_values,
            query_seg,
        )
        return ((inner[0] + grad_keys, inner[1] + grad_values), None)

    carried, ignored = lax.scan(
        gather_one_step, carried, lax.iota(jnp.int32, row_count // gather_block_rows)
    )
    grad_keys_all, grad_values_all = carried
    grad_stack = jnp.stack(
        [
            total_grad.reshape(group_rows, local_width),
            grad_keys_all.reshape(group_rows, local_width),
            grad_values_all.reshape(group_rows, local_width),
        ],
        axis=1,
    )
    grad_stack = grad_stack.astype(jnp.bfloat16).reshape(group_rows, 3, 1, local_width)
    grad_tokens = (
        lax.all_to_all(grad_stack, "head", split_axis=0, concat_axis=2, tiled=True)
        .reshape(rows_dev, 3, all_heads, DH)
        .astype(jnp.float32)
    )
    grad_qkv = jnp.stack(
        [
            rotate(grad_tokens[:, 0], position, -1.0),
            rotate(grad_tokens[:, 1], position, -1.0),
            grad_tokens[:, 2],
        ],
        axis=1,
    )
    grad_qkv = grad_qkv.reshape(rows_dev, 3 * width).astype(jnp.bfloat16)
    grad_wqkv = jnp.dot(input_bf.T, grad_qkv, preferred_element_type=jnp.float32)
    grad_input = jnp.dot(grad_qkv, wqkv_full.T, preferred_element_type=jnp.float32)
    grad_x_ln, grad_gain_one = norm_backward(grad_input, gain_one, normed_one, scale_one)
    dx_out = grad_hidden + grad_x_ln
    summed = (
        lax.psum_scatter(grad_gain_one, ("head", "blk"), scatter_dimension=0, tiled=True),
        lax.psum_scatter(grad_wqkv, ("head", "blk"), scatter_dimension=0, tiled=True),
        lax.psum_scatter(grad_wout, ("head", "blk"), scatter_dimension=0, tiled=True),
        lax.psum_scatter(grad_gain_two, ("head", "blk"), scatter_dimension=0, tiled=True),
        lax.psum_scatter(grad_win, ("head", "blk"), scatter_dimension=0, tiled=True),
        lax.psum_scatter(grad_down, ("head", "blk"), scatter_dimension=1, tiled=True),
    )
    return (y_out, dx_out, summed[0], summed[1], summed[2], summed[3], summed[4], summed[5])


def solution(mesh):
    return jax.shard_map(
        shards,
        mesh=mesh,
        in_specs=(
            P(("head", "blk"), None),
            P(("head", "blk"), None),
            P(),
            P(("head", "blk")),
            P(("head", "blk"), None),
            P(("head", "blk"), None),
            P(("head", "blk")),
            P(("head", "blk"), None),
            P(None, ("head", "blk")),
        ),
        out_specs=(
            P(("head", "blk"), None),
            P(("head", "blk"), None),
            P(("head", "blk")),
            P(("head", "blk"), None),
            P(("head", "blk"), None),
            P(("head", "blk")),
            P(("head", "blk"), None),
            P(None, ("head", "blk")),
        ),
        check_vma=False,
    )
```

profile of v0, /device:TPU:0, one launch (start us, length us, event | category | flops | bytes accessed | tf_op | source)
XLA Modules:
  0.0 1424.9 jit_solution(2221315387794891188)
XLA Ops:
  9.7 43.0 %all-reduce.5 = (bf16[1024]{0:T(1024)(128)(2,1)S(1)}, bf16[1024]{0:T(1024)(128)(2,1)S(1)}) all-reduce(bf16[1024]{0:T(1024)(128)(2,1)S(1)} %dynamic-update-slice, bf16[1024]{0:T(1024)(128)(2,1)S(1)} %dynamic-update-slice.1), channel_id=1, replica_groups=mesh['head'=4,'blk'=8] {'head','blk'}, use_global_device_ids=true, to_apply=%add | all-reduce | flops 2048 | bytes 8192
  58.1 25.4 %all-gather.9.cloned.1.call-done = bf16[1024,3072]{1,0:T(8,128)(2,1)} async-done(((bf16[32,3072]{1,0:T(8,128)(2,1)}), bf16[1024,3072]{1,0:T(8,128)(2,1)}) %all-gather.9.cloned.1.call-update) | async-done | bytes 6291472 | tf_op jit(solution)/shard_map/all_gather | solution.py:120
  83.5 5.5 fusion.107
  89.5 14.1 all_to_all.59
  107.2 69.6 %all-gather.21.cloned.1.call-done = bf16[4096,2,1,256]{3,0,1,2:T(8,128)(2,1)} async-done(((bf16[512,2,1,256]{3,0,1,2:T(8,128)(2,1)}), bf16[4096,2,1,256]{3,0,1,2:T(8,128)(2,1)}) %all-gather.21.cloned.1.call-update) | async-done | bytes 4194320 | tf_op jit(solution)/shard_map/all_gather | solution.py:162
  176.8 6.4 copy.132
  183.2 83.1 %while.39 = (s32[]{:T(128)}, f32[4,512]{1,0:T(4,128)S(1)}, f32[4,512]{1,0:T(4,128)S(1)}, f32[512,4,64]{0,2,1:T(8,128)S(1)}, s32[512]{0:T(512)S(1)}, /*index=5*/s...) while((s32[]{:T(128)}, f32[4,512]{1,0:T(4,128)S(1)}, ...), condition=%wide.region_10.11_spmd.clone, body=%wide.region_7.10_spmd.clone.sunk | while | flops 282734592 | bytes 33431812 | solution.py:174
  188.7 3.4 fusion.166
  209.4 3.4 fusion.166
  230.1 3.4 fusion.166
  250.9 3.4 fusion.166
  267.2 3.4 all-to-all-start.1
  271.8 6.3 all-to-all-done.1
  280.5 46.5 %all-gather.13.cloned.1.call-done = bf16[1024,5248]{1,0:T(8,128)(2,1)} async-done(((bf16[32,5248]{1,0:T(8,128)(2,1)}), bf16[1024,5248]{1,0:T(8,128)(2,1)}) %all-gather.13.cloned.1.call-update) | async-done | bytes 10747920 | tf_op jit(solution)/shard_map/all_gather | solution.py:123
  327.0 7.2 fusion.109
  334.2 60.3 %all-gather.15.cloned.1.call-done = bf16[2624,1024]{0,1:T(8,128)(2,1)} async-done(((bf16[2624,32]{0,1:T(8,128)(2,1)}), bf16[2624,1024]{0,1:T(8,128)(2,1)}) %all-gather.15.cloned.1.call-update) | async-done | bytes 5373968 | tf_op jit(solution)/shard_map/all_gather | solution.py:124
  394.5 7.3 add_convert_fusion
  402.7 4.2 multiply_reduce_fusion
  408.0 9.1 all_to_all.60
  424.6 31.0 %all_gather.42 = f32[4096,4]{0,1:T(4,128)S(1)} all-gather(f32[512,4]{0,1:T(4,128)S(1)} %bitcast.236), channel_id=1, replica_groups=mesh['head'=4,'blk'=8] {'blk'}, dimensions={0}, use_global_device_ids=true | all-gather | bytes 73728 | tf_op jit(solution)/shard_map/all_gather | solution.py:244
  455.6 5.8 fusion.103
  463.5 30.7 %all_gather.44 = f32[4096,4]{0,1:T(4,128)S(1)} all-gather(f32[512,4]{0,1:T(4,128)S(1)} %multiply_reduce_fusion.1), channel_id=1, replica_groups=mesh['head'=4,'blk'=8] {'blk'}, dimensions={0}, use_global_device_ids=true | all-gather | bytes 73728 | tf_op jit(solution)/shard_map/all_gather | solution.py:245
  494.2 82.9 %while.40 = (s32[]{:T(128)}, f32[512,4,64]{0,2,1:T(8,128)}, s32[8]{0:T(128)S(1)}, bf16[4096,2,256]{0,2,1:T(8,128)(2,1)}, s32[512]{0:T(512)S(1)}, /*index=5*/s32[...) while((s32[]{:T(128)}, f32[512,4,64]{0,2,1:T(8,128)}, ...), condition=%wide.region_17.18_spmd.clone, body=%wide.region_16.17_spmd.clone.sunk | while | flops 409600000 | bytes 12345585 | solution.py:238
  499.5 4.9 fusion.175
  509.8 5.0 fusion.175
  520.2 5.0 fusion.175
  530.6 5.1 fusion.175
  541.0 5.0 fusion.175
  551.3 5.0 fusion.175
  561.7 5.0 fusion.175
  572.1 5.0 fusion.175
  578.3 116.8 %while.41 = (s32[]{:T(128)}, f32[512,4,64]{0,2,1:T(8,128)}, f32[512,4,64]{0,2,1:T(8,128)}, s32[8]{0:T(128)S(1)}, bf16[4096,4,64]{0,2,1:T(8,128)(2,1)}, /*index=5...) while((s32[]{:T(128)}, f32[512,4,64]{0,2,1:T(8,128)}, ...), condition=%wide.region_19.20_spmd.clone, body=%wide.region_18.19_spmd.clone.sunk | while | flops 548274176 | bytes 21301032 | solution.py:263
  579.5 3.7 fusion.179
  583.5 4.5 fusion.180
  588.0 4.5 fusion.181
  593.8 3.7 fusion.179
  597.9 4.5 fusion.180
  602.3 4.7 fusion.181
  608.3 3.7 fusion.179
  612.3 4.5 fusion.180
  616.8 4.7 fusion.181
  622.7 3.7 fusion.179
  626.7 4.5 fusion.180
  631.2 4.6 fusion.181
  637.1 3.7 fusion.179
  641.2 4.5 fusion.180
  645.7 4.6 fusion.181
  651.6 3.7 fusion.179
  655.6 4.8 fusion.180
  660.4 4.9 fusion.181
  666.5 3.7 fusion.179
  670.6 4.7 fusion.180
  675.3 4.9 fusion.181
  681.5 3.7 fusion.179
  685.5 4.7 fusion.180
  690.3 4.8 fusion.181
  700.5 24.3 %all_to_all.61 = bf16[512,3,1,256]{3,1,2,0:T(4,128)(2,1)S(1)} all-to-all(bf16[512,3,1,256]{3,1,2,0:T(4,128)(2,1)} %copy.141), channel_id=1, replica_groups=mesh['head'=4,'blk'=8] {'head'}, dimensions={0} | all-to-all | bytes 1572864 | tf_op jit(solution)/shard_map/all_to_all | solution.py:277
  731.8 6.5 fusion.105
  739.4 10.3 fusion.56
  750.3 5.3 fusion.55
  755.7 5.7 fusion.69
  761.4 39.6 %all-reduce.4 = (f32[1024]{0:T(1024)S(1)}, f32[1024]{0:T(1024)S(1)}) all-reduce(f32[1024]{0:T(1024)S(1)} %get-tuple-element.440, f32[1024]{0:T(1024)S(1)} %copy-done.19), channel_id=3, replica_groups=mesh['head'=4,'blk'=8] {'head','blk'}, use_global_device_ids=true, to_apply=%region_23.24.clone | all-reduce | flops 2048 | bytes 16384
  803.2 157.4 %reduce-scatter.5.cloned.1.call-done = f32[32,3072]{1,0:T(8,128)} async-done(((f32[1024,3072]{1,0:T(8,128)}), f32[32,3072]{1,0:T(8,128)}) %reduce-scatter.5.cloned.1.call-update) | async-done | bytes 393232 | tf_op jit(solution)/shard_map/reduce_scatter | solution.py:296
  960.7 457.5 %reduce-scatter.9.cloned.1.call-done = f32[32,5248]{1,0:T(8,128)} async-done(((f32[1024,5248]{1,0:T(8,128)}), f32[32,5248]{1,0:T(8,128)}) %reduce-scatter.9.cloned.1.call-update) | async-done | bytes 671760 | tf_op jit(solution)/shard_map/reduce_scatter | solution.py:299
  (341 shorter events, 153.4 us)
Async XLA Ops:
  7.2 76.3 %all-gather.9.cloned.1.call-start = ((), (), s32[]{:S(2)}) async-start(), calls=%async_computation.8 | async-start | bytes 6488064 | tf_op jit(solution)/shard_map/all_gather | solution.py:120
  7.9 168.9 %all-gather.21.cloned.1.call-start = ((), (), s32[]{:S(2)}) async-start(), calls=%async_computation.18 | async-start | bytes 4718592 | tf_op jit(solution)/shard_map/all_gather | solution.py:162
  104.9 166.9 %all-gather.11.cloned.1.call-start = ((), (), s32[]{:S(2)}) async-start(), calls=%async_computation.9 | async-start | bytes 2162688 | tf_op jit(solution)/shard_map/all_gather | solution.py:121
  105.6 221.4 %all-gather.13.cloned.1.call-start = ((), (), s32[]{:S(2)}) async-start(), calls=%async_computation.10 | async-start | bytes 11083776 | tf_op jit(solution)/shard_map/all_gather | solution.py:123
  106.2 288.3 %all-gather.15.cloned.1.call-start = ((), (), s32[]{:S(2)}) async-start(), calls=%async_computation.11 | async-start | bytes 5677056 | tf_op jit(solution)/shard_map/all_gather | solution.py:124
  188.7 3.5 copy-start
  199.1 3.5 copy-start
  209.4 3.5 copy-start
  219.7 3.5 copy-start
  230.1 3.6 copy-start
  240.5 3.5 copy-start
  250.9 3.5 copy-start
  261.2 3.7 copy-start
  266.3 4.4 copy-start.1
  266.3 13.9 copy-start.11
  266.3 11.8 copy-start.4
  267.2 10.9 all-to-all-start.1
  270.6 307.6 %all-gather.17.cloned.1.call-start = ((), (), s32[]{:S(2)}) async-start(), calls=%async_computation.12 | async-start | bytes 2359296 | tf_op jit(solution)/shard_map/all_gather | solution.py:242
  270.7 184.9 %copy-start.17 = (f32[128]{0:T(128)}, f32[128]{0:T(128)S(1)}, u32[]{:S(2)}) copy-start(f32[128]{0:T(128)S(1)} %compare_convert_fusion) | copy-start | bytes 1540
  271.2 307.0 %all-gather.19.cloned.1.call-start = ((), (), s32[]{:S(2)}) async-start(), calls=%async_computation.13 | async-start | bytes 2359296 | tf_op jit(solution)/shard_map/all_gather | solution.py:243
  280.5 114.0 %copy-start.13 = (bf16[128,1024]{1,0:T(8,128)(2,1)S(1)}, bf16[128,1024]{1,0:T(8,128)(2,1)}, u32[]{:S(2)}) copy-start(bf16[128,1024]{1,0:T(8,128)(2,1)} %param.16) | copy-start | bytes 786436
  394.5 7.3 copy-start.5
  394.5 8.2 copy-start.3
  401.8 0.9 copy-start.14
  402.3 4.5 copy-start.9
  402.7 4.5 copy-start.6
  419.1 384.1 %reduce-scatter.7.cloned.1.call-start = ((), (), s32[]{:S(2)}) async-start(), calls=%async_computation.15 | async-start | bytes 4325376 | tf_op jit(solution)/shard_map/reduce_scatter | solution.py:297
  421.8 381.4 %reduce-scatter.11.cloned.1.call-start = ((), (), s32[]{:S(2)}) async-start(), calls=%async_computation.17 | async-start | bytes 11354112 | tf_op jit(solution)/shard_map/reduce_scatter | solution.py:300
  461.4 1.0 copy-start.12
  461.4 32.8 %copy-start.2 = (bf16[512,4,64]{0,2,1:T(8,128)(2,1)S(1)}, bf16[512,4,64]{0,2,1:T(8,128)(2,1)}, u32[]{:S(2)}) copy-start(bf16[512,4,64]{0,2,1:T(8,128)(2,1)} %copy-done.1) | copy-start | bytes 786436
  461.4 499.2 %reduce-scatter.5.cloned.1.call-start = ((), (), s32[]{:S(2)}) async-start(), calls=%async_computation.14 | async-start | bytes 12976128 | tf_op jit(solution)/shard_map/reduce_scatter | solution.py:296
  579.5 4.0 copy-start.15
  588.0 4.5 copy-start.16
  593.8 4.0 copy-start.15
  602.3 4.7 copy-start.16
  608.2 4.0 copy-start.15
  616.8 4.7 copy-start.16
  622.7 4.0 copy-start.15
  631.2 4.7 copy-start.16
  637.1 4.0 copy-start.15
  645.7 4.7 copy-start.16
  651.6 4.0 copy-start.15
  660.4 4.9 copy-start.16
  666.5 4.0 copy-start.15
  675.3 4.9 copy-start.16
  681.5 4.0 copy-start.15
  690.3 4.8 copy-start.16
  730.9 0.9 copy-start.7
  738.3 1.1 copy-start.10
  738.3 679.9 %reduce-scatter.9.cloned.1.call-start = ((), (), s32[]{:S(2)}) async-start(), calls=%async_computation.16 | async-start | bytes 22167552 | tf_op jit(solution)/shard_map/reduce_scatter | solution.py:299
  749.7 0.7 copy-start.18
  750.3 5.3 copy-start.8
  755.7 5.8 copy-start.19
Sparse Core Ops, SparseCore 0:
  10.9 72.5 all-gather.8
  105.0 71.7 all-gather.20
  179.8 54.8 all-gather.10
  237.4 89.5 all-gather.12
  329.8 64.6 all-gather.14
  397.0 50.7 all-gather.16
  449.8 50.5 all-gather.18
  503.3 141.4 reduce-scatter.6
  651.3 148.2 reduce-scatter.10
  806.0 154.5 reduce-scatter.4
  963.6 454.4 reduce-scatter.8
where the time goes:
time: 1430 us; the launch traced here: 1420 us
  waiting for transfers between devices  826 us (58%)
  matrix products  263 us (18%)
  blocking collectives  192 us (13%)
  local copies, waits for them, and re-layouts  61.3 us (4%)
  other arithmetic  46.9 us (3%)
  loops' own time  16.5 us (1%)
  between operations  14.6 us (1%)
    reduce_scatter x1, waiting for transfers between devices, shards(): lax.psum_scatter(grad_win, ('head', 'blk'), scatter_dimension=0, tiled=True)  458 us
    reduce_scatter x1, waiting for transfers between devices, shards(): lax.psum_scatter(grad_wqkv, ('head', 'blk'), scatter_dimension=0, tiled=T...  157 us
    unnamed x2, blocking collectives  82.6 us
    all_gather x1, waiting for transfers between devices, shards(): key_part = lax.all_gather(key_value, 'blk', axis=0, tiled=True)  69.6 us
    all_gather x1, waiting for transfers between devices, shards(): lax.all_gather(w_mlp_out, ('head', 'blk'), axis=1, tiled=True)  60.3 us
    dot_general x16, matrix products, score_grads(): jnp.einsum('qhd,khd->hqk', query_in, key_in, preferred_element_type=jnp.f...  51.3 us
    all_gather x1, waiting for transfers between devices, shards(): lax.all_gather(w_in, ('head', 'blk'), axis=0, tiled=True)  46.5 us
    dot_general x8, matrix products, query_one_step(): jnp.einsum('hqk,khd->qhd', grad_scores, keys_in, preferred_element_type=j...  40.1 us
  transfers between devices with their start and end apart: 12, of which 7 were waited for; matrix products, arithmetic and copies ran while one was open for 25% of the time, Pallas kernels for 0%

commit v1 on v0

--- a/solution.py
+++ b/solution.py
@@ -115,13 +115,30 @@
     local_width = local_heads * DH
     group_rows = head_groups * rows_dev
     nseq_count = lengths.shape[0]
+
+    def search_spots(shard_in, link_axis):
+        y_new = lax.axis_size(link_axis)
+        response = lax.axis_index(link_axis)
+        reached, z = (y_new, response)
+        opened, f_now = (shard_in, 1)
+        while f_now < reached:
+            history = []
+            for p in range(reached):
+                history.append((p, p ^ f_now))
+            item_now = lax.ppermute(opened, link_axis, history)
+            local_now = jnp.concatenate([opened, item_now], axis=1)
+            r_now = jnp.concatenate([item_now, opened], axis=1)
+            opened = jnp.where(z & f_now == 0, local_now, r_now)
+            f_now = 2 * f_now
+        return opened
+
     gain_one, wqkv_full, wout_full, gain_two, win_full, wdown_full = (
         lax.all_gather(ln_attn, ("head", "blk"), axis=0, tiled=True),
         lax.all_gather(w_qkv, ("head", "blk"), axis=0, tiled=True),
         lax.all_gather(w_attn_out, ("head", "blk"), axis=0, tiled=True),
         lax.all_gather(ln_mlp, ("head", "blk"), axis=0, tiled=True),
         lax.all_gather(w_in, ("head", "blk"), axis=0, tiled=True),
-        lax.all_gather(w_mlp_out, ("head", "blk"), axis=1, tiled=True),
+        search_spots(w_mlp_out, ("head", "blk")),
     )
     gain_one = gain_one.astype(jnp.float32)
     gain_two = gain_two.astype(jnp.float32)

time: 1430 us -> 1390 us (0.972)
  waiting for transfers between devices: 826 us -> 755 us
  local copies, waits for them, and re-layouts: 61.3 us -> 99.6 us
    ppermute x0 -> x5, waiting for transfers between devices: none -> 74 us  [search_spots(): item_now = lax.ppermute(opened, link_axis, history)]
    all_gather x1, waiting for transfers between devices: 69.6 us -> 2.16 us  [shards(): key_part = lax.all_gather(key_value, 'blk', axis=0, tiled=True)]
    all_gather x1 -> x0, waiting for transfers between devices: 60.3 us -> none  [shards(): lax.all_gather(w_mlp_out, ('head', 'blk'), axis=1, tiled=True)]
    dynamic_slice x24, local copies, waits for them, and re-layouts: 1.81 us -> 18 us  [take_rows(): lax.dynamic_slice_in_dim(array_in, block_at * block_rows, block_rows, 0)]
  transfers between devices with their start and end apart: 12 -> 16, of which waited for: 7 -> 10; matrix products, arithmetic and copies ran while one was open for 25% -> 27% of each run, Pallas kernels for 0% -> 0%
where the time goes in v1:
time: 1390 us; the launch traced here: 1380 us
  waiting for transfers between devices  755 us (54%)
  matrix products  249 us (18%)
  blocking collectives  189 us (14%)
  local copies, waits for them, and re-layouts  99.6 us (7%)
  other arithmetic  50.1 us (4%)
  loops' own time  16.3 us (1%)
  between operations  15.3 us (1%)
    reduce_scatter x1, waiting for transfers between devices, shards(): lax.psum_scatter(grad_win, ('head', 'blk'), scatter_dimension=0, tiled=True)  457 us
    reduce_scatter x1, waiting for transfers between devices, shards(): lax.psum_scatter(grad_wqkv, ('head', 'blk'), scatter_dimension=0, tiled=T...  147 us
    unnamed x2, blocking collectives  80.5 us
    ppermute x5, waiting for transfers between devices, search_spots(): item_now = lax.ppermute(opened, link_axis, history)  74 us
    dot_general x16, matrix products, score_grads(): jnp.einsum('qhd,khd->hqk', query_in, key_in, preferred_element_type=jnp.f...  51.6 us
    all_gather x1, waiting for transfers between devices, shards(): lax.all_gather(w_in, ('head', 'blk'), axis=0, tiled=True)  46.5 us
    dot_general x8, matrix products, query_one_step(): jnp.einsum('hqk,khd->qhd', grad_scores, keys_in, preferred_element_type=j...  39.6 us
    dot_general x8, matrix products, key_grad_rows(): jnp.einsum('hqk,qhd->khd', grad_scores, query_in, preferred_element_type=...  36.2 us
  transfers between devices with their start and end apart: 16, of which 10 were waited for; matrix products, arithmetic and copies ran while one was open for 27% of the time, Pallas kernels for 0%

profile of v1, /device:TPU:0, one launch (start us, length us, event | category | flops | bytes accessed | tf_op | source)
XLA Modules:
  0.0 1383.1 jit_solution(16577572526171363719)
XLA Ops:
  9.7 43.0 %all-reduce.5 = (bf16[1024]{0:T(1024)(128)(2,1)S(1)}, bf16[1024]{0:T(1024)(128)(2,1)S(1)}) all-reduce(bf16[1024]{0:T(1024)(128)(2,1)S(1)} %dynamic-update-slice, bf16[1024]{0:T(1024)(128)(2,1)S(1)} %dynamic-update-slice.1), channel_id=1, replica_groups=mesh['head'=4,'blk'=8] {'head','blk'}, use_global_device_ids=true, to_apply=%add | all-reduce | flops 2048 | bytes 8192
  58.7 24.8 %all-gather.8.cloned.1.call-done = bf16[1024,3072]{1,0:T(8,128)(2,1)} async-done(((bf16[32,3072]{1,0:T(8,128)(2,1)}), bf16[1024,3072]{1,0:T(8,128)(2,1)}) %all-gather.8.cloned.1.call-update) | async-done | bytes 6291472 | tf_op jit(solution)/shard_map/all_gather | solution.py:137
  83.5 5.5 fusion.109
  89.6 14.1 %all_to_all.59 = bf16[128,3,4,256]{0,3,1,2:T(8,128)(2,1)S(1)} all-to-all(bf16[128,3,4,256]{0,3,1,2:T(8,128)(2,1)S(1)} %copy.144), channel_id=1, replica_groups=mesh['head'=4,'blk'=8] {'head'}, dimensions={2} | all-to-all | bytes 1572864 | tf_op jit(solution)/shard_map/all_to_all | solution.py:167
  107.9 4.3 collective-permute-done
  113.9 22.6 %collective-permute-done.1 = bf16[2624,64]{0,1:T(8,128)(2,1)S(1)} collective-permute-done((bf16[2624,64]{0,1:T(8,128)(2,1)S(1)}, bf16[2624,64]{0,1:T(8,128)(2,1)S(1)}, u32[]{:S(2)}, u32[]{:S(2)}) %collective-permute-start.1) | collective-permute-done | bytes 335904 | tf_op jit(solution)/shard_map/ppermute | solution.py:128
  137.0 44.8 %collective-permute-done.2 = bf16[2624,128]{1,0:T(8,128)(2,1)S(1)} collective-permute-done((bf16[2624,128]{1,0:T(8,128)(2,1)S(1)}, bf16[2624,128]{1,0:T(8,128)(2,1)S(1)}, u32[]{:S(2)}, u32[]{:S(2)}) %collective-permute-start.2) | collective-permute-done | bytes 671776 | tf_op jit(solution)/shard_map/ppermute | solution.py:128
  188.3 4.3 maximum_select_fusion.1
  192.6 4.6 copy.155
  200.9 6.5 copy.147
  207.3 88.5 %while.39 = (s32[]{:T(128)}, f32[4,512]{1,0:T(4,128)S(1)}, f32[4,512]{1,0:T(4,128)S(1)}, f32[512,4,64]{0,2,1:T(8,128)S(1)}, s32[512]{0:T(512)S(1)}, /*index=5*/s...) while((s32[]{:T(128)}, f32[4,512]{1,0:T(4,128)S(1)}, ...), condition=%wide.region_10.11_spmd.clone, body=%wide.region_7.10_spmd.clone.sunk | while | flops 282734592 | bytes 33431812 | solution.py:191
  257.6 3.4 fusion.166
  290.7 3.7 fusion.166
  296.8 3.4 all-to-all-start.1
  300.3 4.5 copy.156
  309.4 46.5 %all-gather.12.cloned.1.call-done = bf16[1024,5248]{1,0:T(8,128)(2,1)} async-done(((bf16[32,5248]{1,0:T(8,128)(2,1)}), bf16[1024,5248]{1,0:T(8,128)(2,1)}) %all-gather.12.cloned.1.call-update) | async-done | bytes 10747920 | tf_op jit(solution)/shard_map/all_gather | solution.py:140
  355.9 5.9 fusion.111
  361.8 6.0 add_convert_fusion
  369.0 4.2 multiply_reduce_fusion
  374.4 8.5 all_to_all.60
  390.4 30.9 %all_gather.38 = f32[4096,4]{0,1:T(4,128)S(1)} all-gather(f32[512,4]{0,1:T(4,128)S(1)} %bitcast.238), channel_id=1, replica_groups=mesh['head'=4,'blk'=8] {'blk'}, dimensions={0}, use_global_device_ids=true | all-gather | bytes 73728 | tf_op jit(solution)/shard_map/all_gather | solution.py:261
  421.3 5.7 fusion.106
  428.3 32.7 %all_gather.40 = f32[4096,4]{0,1:T(4,128)} all-gather(f32[512,4]{0,1:T(4,128)S(1)} %multiply_reduce_fusion.1), channel_id=1, replica_groups=mesh['head'=4,'blk'=8] {'blk'}, dimensions={0}, use_global_device_ids=true | all-gather | bytes 73728 | tf_op jit(solution)/shard_map/all_gather | solution.py:262
  460.9 87.0 %while.40 = (s32[]{:T(128)}, f32[512,4,64]{0,2,1:T(8,128)}, s32[8]{0:T(128)S(1)}, bf16[4096,2,256]{0,2,1:T(8,128)(2,1)}, s32[512]{0:T(512)S(1)}, /*index=5*/s32[...) while((s32[]{:T(128)}, f32[512,4,64]{0,2,1:T(8,128)}, ...), condition=%wide.region_17.18_spmd.clone, body=%wide.region_16.17_spmd.clone.sunk | while | flops 409600000 | bytes 12345585 | solution.py:255
  466.9 4.8 fusion.175
  477.6 5.0 fusion.175
  488.6 4.9 fusion.175
  499.4 5.0 fusion.175
  510.3 5.0 fusion.175
  521.2 5.0 fusion.175
  532.1 4.9 fusion.175
  543.0 5.0 fusion.175
  549.1 125.4 %while.41 = (s32[]{:T(128)}, f32[512,4,64]{0,2,1:T(8,128)S(1)}, f32[512,4,64]{0,2,1:T(8,128)}, s32[8]{0:T(128)S(1)}, bf16[4096,4,64]{0,2,1:T(8,128)(2,1)}, /*ind...) while((s32[]{:T(128)}, f32[512,4,64]{0,2,1:T(8,128)S(1)}, ...), condition=%wide.region_19.20_spmd.clone, body=%wide.region_18.19_spmd.clone.sunk | while | flops 548274176 | bytes 22349636 | solution.py:280
  550.4 3.7 fusion.179
  555.8 4.4 fusion.180
  560.3 3.6 fusion.181
  565.9 3.7 fusion.179
  571.3 4.4 fusion.180
  575.8 3.6 fusion.181
  581.4 3.7 fusion.179
  586.9 4.5 fusion.180
  591.4 3.6 fusion.181
  597.0 3.7 fusion.179
  602.4 4.5 fusion.180
  606.9 3.6 fusion.181
  612.5 3.7 fusion.179
  617.9 4.7 fusion.180
  622.6 3.8 fusion.181
  628.5 3.7 fusion.179
  633.9 4.7 fusion.180
  638.6 3.8 fusion.181
  644.5 3.7 fusion.179
  650.0 4.6 fusion.180
  654.6 3.6 fusion.181
  660.2 3.7 fusion.179
  665.7 4.4 fusion.180
  670.1 3.6 fusion.181
  678.2 22.5 %all_to_all.61 = bf16[512,3,1,256]{3,1,2,0:T(4,128)(2,1)S(1)} all-to-all(bf16[512,3,1,256]{3,1,2,0:T(4,128)(2,1)S(1)} %copy.165), channel_id=1, replica_groups=mesh['head'=4,'blk'=8] {'head'}, dimensions={0} | all-to-all | bytes 1572864 | tf_op jit(solution)/shard_map/all_to_all | solution.py:294
  705.3 6.5 fusion.107
  713.1 9.2 fusion.57
  722.9 7.3 fusion.55
  732.5 37.4 %all-reduce.4 = (f32[1024]{0:T(1024)S(1)}, f32[1024]{0:T(1024)S(1)}) all-reduce(f32[1024]{0:T(1024)S(1)} %get-tuple-element.440, f32[1024]{0:T(1024)S(1)} %copy-done.42), channel_id=3, replica_groups=mesh['head'=4,'blk'=8] {'head','blk'}, use_global_device_ids=true, to_apply=%region_23.24.clone | all-reduce | flops 2048 | bytes 16384
  772.2 146.5 %reduce-scatter.5.cloned.1.call-done = f32[32,3072]{1,0:T(8,128)} async-done(((f32[1024,3072]{1,0:T(8,128)}), f32[32,3072]{1,0:T(8,128)}) %reduce-scatter.5.cloned.1.call-update) | async-done | bytes 393232 | tf_op jit(solution)/shard_map/reduce_scatter | solution.py:313
  918.7 457.3 %reduce-scatter.9.cloned.1.call-done = f32[32,5248]{1,0:T(8,128)} async-done(((f32[1024,5248]{1,0:T(8,128)}), f32[32,5248]{1,0:T(8,128)}) %reduce-scatter.9.cloned.1.call-update) | async-done | bytes 671760 | tf_op jit(solution)/shard_map/reduce_scatter | solution.py:316
  (442 shorter events, 200.1 us)
Async XLA Ops:
  7.2 76.4 %all-gather.8.cloned.1.call-start = ((), (), s32[]{:S(2)}) async-start(), calls=%async_computation.8 | async-start | bytes 6488064 | tf_op jit(solution)/shard_map/all_gather | solution.py:137
  7.9 192.9 %all-gather.18.cloned.1.call-start = ((), (), s32[]{:S(2)}) async-start(), calls=%async_computation.17 | async-start | bytes 4718592 | tf_op jit(solution)/shard_map/all_gather | solution.py:179
  52.7 36.4 %copy-start.26 = (f32[1024]{0:T(1024)}, f32[1024]{0:T(1024)S(1)}, u32[]{:S(2)}) copy-start(f32[1024]{0:T(1024)S(1)} %convert_element_type.125) | copy-start | bytes 12292
  53.5 4.4 copy-start.45
  56.8 32.3 %copy-start.35 = (f32[128]{0:T(128)}, f32[128]{0:T(128)S(1)}, u32[]{:S(2)}) copy-start(f32[128]{0:T(128)S(1)} %broadcast_multiply_fusion.6) | copy-start | bytes 1540
  57.9 31.1 %copy-start.39 = (f32[128]{0:T(128)}, f32[128]{0:T(128)S(1)}, u32[]{:S(2)}) copy-start(f32[128]{0:T(128)S(1)} %add_rsqrt_fusion.1) | copy-start | bytes 1540
  58.7 30.5 %copy-start.30 = (f32[128,32]{0,1:T(8,128)}, f32[128,32]{0,1:T(8,128)S(1)}, u32[]{:S(2)}) copy-start(f32[128,32]{0,1:T(8,128)S(1)} %get-tuple-element.546) | copy-start | bytes 49156
  105.1 200.0 %all-gather.10.cloned.1.call-start = ((), (), s32[]{:S(2)}) async-start(), calls=%async_computation.9 | async-start | bytes 2162688 | tf_op jit(solution)/shard_map/all_gather | solution.py:138
  105.9 250.1 %all-gather.12.cloned.1.call-start = ((), (), s32[]{:S(2)}) async-start(), calls=%async_computation.10 | async-start | bytes 11083776 | tf_op jit(solution)/shard_map/all_gather | solution.py:140
  106.4 5.8 collective-permute-start
  112.3 24.2 %collective-permute-start.1 = (bf16[2624,64]{0,1:T(8,128)(2,1)S(1)}, bf16[2624,64]{0,1:T(8,128)(2,1)S(1)}, u32[]{:S(2)}, u32[]{:S(2)}) collective-permute-start(bf16[2624,64]{0,1:T(8,128)(2,1)S(1)} %maximum_select_fusion.6), channel_id=1, source_target_pairs={{0,2},{1,3},{2,0},{3,1},{4,6},{5,7},{6,4},{7,5},{8,10},{9,11},{10,... | collective-permute-start | bytes 1007624 | tf_op jit(solution)/shard_map/ppermute | solution.py:128
  136.9 44.9 %collective-permute-start.2 = (bf16[2624,128]{1,0:T(8,128)(2,1)S(1)}, bf16[2624,128]{1,0:T(8,128)(2,1)S(1)}, u32[]{:S(2)}, u32[]{:S(2)}) collective-permute-start(bf16[2624,128]{1,0:T(8,128)(2,1)S(1)} %copy.149), channel_id=1, source_target_pairs={{0,4},{1,5},{2,6},{3,7},{4,0},{5,1},{6,2},{7,3},{8,12},{9,13},{10,... | collective-permute-start | bytes 2015240 | tf_op jit(solution)/shard_map/ppermute | solution.py:128
  183.3 3.3 collective-permute-start.3
  197.2 103.1 %collective-permute-start.4 = (bf16[2624,512]{1,0:T(8,128)(2,1)}, bf16[2624,512]{1,0:T(8,128)(2,1)}, u32[]{:S(2)}, u32[]{:S(2)}) collective-permute-start(bf16[2624,512]{1,0:T(8,128)(2,1)} %copy.155), channel_id=1, source_target_pairs={{0,16},{1,17},{2,18},{3,19},{4,20},{5,21},{6,22},{7,23},{8,24},{9,... | collective-permute-start | bytes 8060936 | tf_op jit(solution)/shard_map/ppermute | solution.py:128
  200.8 6.5 copy-start.14
  200.9 6.5 copy-start.21
  257.6 3.5 copy-start
  290.7 3.7 copy-start
  295.8 9.0 copy-start.1
  295.9 9.0 copy-start.15
  295.9 4.4 copy-start.48
  296.8 10.2 all-to-all-start.1
  300.2 248.9 %all-gather.14.cloned.1.call-start = ((), (), s32[]{:S(2)}) async-start(), calls=%async_computation.11 | async-start | bytes 2359296 | tf_op jit(solution)/shard_map/all_gather | solution.py:259
  300.3 121.0 %copy-start.43 = (f32[128]{0:T(128)}, f32[128]{0:T(128)S(1)}, u32[]{:S(2)}) copy-start(f32[128]{0:T(128)S(1)} %compare_convert_fusion) | copy-start | bytes 1540
  300.3 6.7 copy-start.3
  304.9 244.2 %all-gather.16.cloned.1.call-start = ((), (), s32[]{:S(2)}) async-start(), calls=%async_computation.12 | async-start | bytes 2359296 | tf_op jit(solution)/shard_map/all_gather | solution.py:260
  309.2 64.0 %copy-start.33 = (f32[128]{0:T(128)}, f32[128]{0:T(128)S(1)}, u32[]{:S(2)}) copy-start(f32[128]{0:T(128)S(1)} %broadcast_multiply_fusion.5) | copy-start | bytes 1540
  309.4 63.8 %copy-start.37 = (f32[128]{0:T(128)}, f32[128]{0:T(128)S(1)}, u32[]{:S(2)}) copy-start(f32[128]{0:T(128)S(1)} %add_rsqrt_fusion) | copy-start | bytes 1540
  309.4 52.4 %copy-start.17 = (bf16[128,1024]{1,0:T(8,128)(2,1)S(1)}, bf16[128,1024]{1,0:T(8,128)(2,1)}, u32[]{:S(2)}) copy-start(bf16[128,1024]{1,0:T(8,128)(2,1)} %param.16) | copy-start | bytes 786436
  355.9 5.9 copy-start.4
  355.9 5.9 copy-start.11
  355.9 12.6 slice-start.2
  361.8 6.7 slice-start.3
  361.8 6.7 slice-start.4
  368.5 4.7 copy-start.9
  368.5 52.8 %copy-start.8 = (bf16[128,2624]{1,0:T(8,128)(2,1)}, bf16[128,2624]{1,0:T(8,128)(2,1)S(1)}, u32[]{:S(2)}) copy-start(bf16[128,2624]{1,0:T(8,128)(2,1)S(1)} %get-tuple-element.523) | copy-start | bytes 2015236
  369.0 4.5 copy-start.5
  383.9 388.3 %reduce-scatter.7.cloned.1.call-start = ((), (), s32[]{:S(2)}) async-start(), calls=%async_computation.14 | async-start | bytes 4325376 | tf_op jit(solution)/shard_map/reduce_scatter | solution.py:314
  386.6 34.7 %copy-start.18 = (bf16[128,1024]{1,0:T(8,128)(2,1)S(1)}, bf16[128,1024]{1,0:T(8,128)(2,1)}, u32[]{:S(2)}) copy-start(bf16[128,1024]{1,0:T(8,128)(2,1)} %param.16) | copy-start | bytes 786436
  386.7 385.5 %reduce-scatter.11.cloned.1.call-start = ((), (), s32[]{:S(2)}) async-start(), calls=%async_computation.16 | async-start | bytes 11354112 | tf_op jit(solution)/shard_map/reduce_scatter | solution.py:317
  427.0 33.9 %copy-start.2 = (bf16[512,4,64]{0,2,1:T(8,128)(2,1)S(1)}, bf16[512,4,64]{0,2,1:T(8,128)(2,1)}, u32[]{:S(2)}) copy-start(bf16[512,4,64]{0,2,1:T(8,128)(2,1)} %copy-done.1) | copy-start | bytes 786436
  427.1 491.6 %reduce-scatter.5.cloned.1.call-start = ((), (), s32[]{:S(2)}) async-start(), calls=%async_computation.13 | async-start | bytes 12976128 | tf_op jit(solution)/shard_map/reduce_scatter | solution.py:313
  460.9 88.2 %copy-start.22 = (f32[512,4,64]{0,2,1:T(8,128)S(1)}, f32[512,4,64]{0,2,1:T(8,128)}, u32[]{:S(2)}) copy-start(f32[512,4,64]{0,2,1:T(8,128)} %custom-call.4) | copy-start | bytes 1572868
  550.4 5.4 copy-start.28
  555.8 4.5 copy-start.24
  565.9 5.4 copy-start.28
  571.3 4.5 copy-start.24
  581.4 5.4 copy-start.28
  586.9 4.5 copy-start.24
  597.0 5.4 copy-start.28
  602.4 4.5 copy-start.24
  612.5 5.4 copy-start.28
  617.9 4.7 copy-start.24
  628.5 5.4 copy-start.28
  633.9 4.7 copy-start.24
  644.5 5.5 copy-start.28
  650.0 4.6 copy-start.24
  660.2 5.4 copy-start.28
  665.6 4.4 copy-start.24
  711.8 664.2 %reduce-scatter.9.cloned.1.call-start = ((), (), s32[]{:S(2)}) async-start(), calls=%async_computation.15 | async-start | bytes 22167552 | tf_op jit(solution)/shard_map/reduce_scatter | solution.py:316
  722.2 8.0 slice-start
  722.9 7.3 slice-start.1
  722.9 7.3 copy-start.7
  722.9 7.3 copy-start.41
  (34 other events, 50.9 us)
Sparse Core Ops, SparseCore 0:
  10.9 72.5 all-gather.7
  105.2 95.5 all-gather.17
  203.8 59.7 all-gather.9
  266.3 89.5 all-gather.11
  358.4 50.0 all-gather.13
  410.4 49.7 all-gather.15
  463.1 142.1 reduce-scatter.6
  611.8 145.7 reduce-scatter.10
  764.2 154.4 reduce-scatter.4
  921.5 454.4 reduce-scatter.8
